TPU v7x, 32 devices: a whole 2x2x4 slice. The times are simulated.
32 devices in a mesh: dp: 16 (over z, y, x), tensor: 2 (over core).
Axes of the slice: x: 2, y: 2, z: 4, core: 2. Of those that a mesh axis runs over, the one named last changes fastest.
Arguments:
- tokens: bfloat16 [24576, 768], P(('dp', 'tensor')), may hold values from -6 to 6
- kept_patches: int32 [24576], P(('dp', 'tensor')), may hold values from 0 to 1567, as said below
- clip_lengths: int32 [128], replicated, may hold values from 39 to 314, as said below
- clip_device: int32 [128], replicated, may hold values from 0 to 31, as said below
- cot_output: bfloat16 [24576, 768], P(('dp', 'tensor')), may hold values from -6 to 6
- cot_aligned: bfloat16 [24576, 1024], P(('dp', 'tensor')), may hold values from -6 to 6
- entry_weight: float32 [1769472], P(('dp', 'tensor')), may hold values from -0.21875 to 0.21875
- entry_first: float32 [1769472], P(('dp', 'tensor')), may hold values from -112 to 112
- entry_second: float32 [1769472], P(('dp', 'tensor')), may hold values from 245.76 to 4096.8193
- exit_weight: float32 [589824], P(('dp', 'tensor')), may hold values from -1.75 to 1.75
- exit_first: float32 [589824], P(('dp', 'tensor')), may hold values from -24 to 24
- exit_second: float32 [589824], P(('dp', 'tensor')), may hold values from 12.288 to 204.71808
- align_weight: float32 [786432], P(('dp', 'tensor')), may hold values from -0.21875 to 0.21875
- align_first: float32 [786432], P(('dp', 'tensor')), may hold values from -128 to 128
- align_second: float32 [786432], P(('dp', 'tensor')), may hold values from 447.2832 to 8183.808
- expand_weight: float32 [3072, 768], P(('dp', 'tensor')), may hold values from -0.21875 to 0.21875
- expand_first: float32 [3072, 768], P(('dp', 'tensor')), may hold values from -32 to 32
- expand_second: float32 [3072, 768], P(('dp', 'tensor')), may hold values from 24.576 to 409.68192
- reduce_weight: float32 [3072, 768], P(('dp', 'tensor')), may hold values from -0.109375 to 0.109375
- reduce_first: float32 [3072, 768], P(('dp', 'tensor')), may hold values from -80 to 80
- reduce_second: float32 [3072, 768], P(('dp', 'tensor')), may hold values from 144.50688 to 2457.6
- position_table: float32 [1204224], P(('dp', 'tensor')), may hold values from -3 to 3
- position_first: float32 [1204224], P(('dp', 'tensor')), may hold values from -5 to 5
- position_second: float32 [1204224], P(('dp', 'tensor')), may hold values from 0.5219265 to 7.836735
- norm_params: float32 [3072], P(('dp', 'tensor')), may hold values from -1.5 to 1.5, as said below
- norm_first: float32 [3072], P(('dp', 'tensor')), may hold values from -128 to 128
- norm_second: float32 [3072], P(('dp', 'tensor')), may hold values from 447.2832 to 8183.808
Outputs:
- block_out: bfloat16 [24576, 768], P(('dp', 'tensor'))
- aligned: bfloat16 [24576, 1024], P(('dp', 'tensor'))
- token_grad: float32 [24576, 768], P(('dp', 'tensor'))
- new_entry_first: float32 [1769472], P(('dp', 'tensor'))
- new_entry_second: float32 [1769472], P(('dp', 'tensor'))
- new_entry_weight: float32 [1769472], P(('dp', 'tensor'))
- new_exit_first: float32 [589824], P(('dp', 'tensor'))
- new_exit_second: float32 [589824], P(('dp', 'tensor'))
- new_exit_weight: float32 [589824], P(('dp', 'tensor'))
- new_align_first: float32 [786432], P(('dp', 'tensor'))
- new_align_second: float32 [786432], P(('dp', 'tensor'))
- new_align_weight: float32 [786432], P(('dp', 'tensor'))
- new_expand_first: float32 [3072, 768], P(('dp', 'tensor'))
- new_expand_second: float32 [3072, 768], P(('dp', 'tensor'))
- new_expand_weight: float32 [3072, 768], P(('dp', 'tensor'))
- new_reduce_first: float32 [3072, 768], P(('dp', 'tensor'))
- new_reduce_second: float32 [3072, 768], P(('dp', 'tensor'))
- new_reduce_weight: float32 [3072, 768], P(('dp', 'tensor'))
- new_position_first: float32 [1204224], P(('dp', 'tensor'))
- new_position_second: float32 [1204224], P(('dp', 'tensor'))
- new_position_table: float32 [1204224], P(('dp', 'tensor'))
- new_norm_first: float32 [3072], P(('dp', 'tensor'))
- new_norm_second: float32 [3072], P(('dp', 'tensor'))
- new_norm_params: float32 [3072], P(('dp', 'tensor'))
- lamb_stats: float32 [3, 7], replicated
Inputs may be any that keep to these rules, and one draw needn't show every extreme that they name: `clip_lengths`: every clip has 314 rows (a video clip) or 39 rows (an image). `clip_device`: each device index d = i * 2 + j holds exactly 4 clips, at most 2 of them video clips, and some device holds 2. `kept_patches`: within a video clip the rows hold distinct positions below 1568 in rising order, within an image distinct positions below 196 in rising order; padding rows hold 0. `norm_params`: gains lie in 0.5 to 1.5; shifts are normal of deviation 0.5, held within -1.5 to 1.5.
All inputs are finite; a program needn't handle non-finite values.
Results may differ from a plain program's by a relative error of at most 0.0085.
The roundings to bfloat16 on the way count: a program that leaves them out, or rounds other values in their place, can miss the bound.
Values may be sent and summed in bfloat16 or wider, within the bound.
A program may use at most 192 MiB of HBM per device.

v0:
```python
import jax
import jax.numpy as jnp
from jax import lax
from jax.sharding import PartitionSpec as P

H = 12
HD = 64
LN_EPS = 1e-06
MASKED = -1e30
RATE = 0.5
BETA_ONE = 0.9
BETA_TWO = 0.98
ADAM_EPS = 1e-06
DECAY = 0.05
TINY = 1e-06


def contract(left, right, left_dim, right_dim):
    return lax.dot_general(
        left, right, (((left_dim,), (right_dim,)), ((), ())), preferred_element_type=jnp.float32
    )


def layer_norm(values, gain, shift):
    center = values - jnp.mean(values, axis=-1, keepdims=True)
    spread = jnp.mean(center * center, axis=-1, keepdims=True)
    return center * lax.rsqrt(spread + LN_EPS) * gain + shift


def gelu_exact(values):
    return jax.nn.gelu(values, approximate=False)


def row_layout(clip_lengths, clip_device, device, row_count):
    mine = clip_device == device
    own_length = jnp.where(mine, clip_lengths, 0)
    starts = jnp.cumsum(own_length) - own_length
    filled = jnp.sum(own_length)
    positions = jnp.arange(row_count, dtype=jnp.int32)
    begun = mine[None, :] & (starts[None, :] <= positions[:, None])
    segment = jnp.sum(begun.astype(jnp.int32), axis=1)
    valid_rows = positions < filled
    return (jnp.where(valid_rows, segment, 0), valid_rows)


def head_scores(queries, key_rows, same_clip, score_scale):
    scores = contract(queries, key_rows, 1, 1) * score_scale
    return jnp.where(same_clip, scores, MASKED)


def head_forward(queries, key_rows, value_rows, same_clip, score_scale):
    scores = head_scores(queries, key_rows, same_clip, score_scale)
    peak_score = jnp.max(scores, axis=1, keepdims=True)
    raised = jnp.exp(scores - peak_score)
    row_total = jnp.sum(raised, axis=1, keepdims=True)
    attention = raised / row_total
    result = jnp.dot(attention.astype(jnp.bfloat16), value_rows, preferred_element_type=jnp.float32)
    return (result, (peak_score + jnp.log(row_total))[:, 0])


def head_backward(queries, key_rows, value_rows, log_total, grad_heads, same_clip, score_scale):
    scores = head_scores(queries, key_rows, same_clip, score_scale)
    attention = jnp.exp(scores - log_total[:, None])
    attention_low = attention.astype(jnp.bfloat16)
    grad_values = contract(attention_low, grad_heads, 0, 0)
    grad_attention = contract(grad_heads, value_rows, 1, 1)
    inner = jnp.sum(attention * grad_attention, axis=1, keepdims=True)
    grad_score = (attention * (grad_attention - inner)).astype(jnp.bfloat16)
    grad_queries = jnp.dot(grad_score, key_rows, preferred_element_type=jnp.float32) * score_scale
    grad_keys = contract(grad_score, queries, 0, 0) * score_scale
    return (grad_queries, grad_keys, grad_values)


def lamb_moments(weight, gradient, first, second, decay):
    new_first = BETA_ONE * first + (1.0 - BETA_ONE) * gradient
    new_second = BETA_TWO * second + (1.0 - BETA_TWO) * gradient * gradient
    update = new_first / (jnp.sqrt(new_second) + ADAM_EPS) + decay * weight
    return (new_first, new_second, update)


def local(
    tokens,
    kept_patches,
    clip_lengths,
    clip_device,
    cot_output,
    cot_aligned,
    entry_weight,
    entry_first,
    entry_second,
    exit_weight,
    exit_first,
    exit_second,
    align_weight,
    align_first,
    align_second,
    expand_weight,
    expand_first,
    expand_second,
    reduce_weight,
    reduce_first,
    reduce_second,
    position_table,
    position_first,
    position_second,
    norm_params,
    norm_first,
    norm_second,
):
    row_count, model_width = tokens.shape
    align_width = cot_aligned.shape[1]
    score_scale = HD ** (-0.5)
    masters = (
        entry_weight,
        exit_weight,
        align_weight,
        expand_weight,
        reduce_weight,
        position_table,
        norm_params,
    )
    device = lax.axis_index("dp") * lax.axis_size("tensor") + lax.axis_index("tensor")
    segment, valid_rows = row_layout(clip_lengths, clip_device, device, row_count)
    same_clip = segment[:, None] == segment[None, :]
    valid_column = valid_rows[:, None]
    gathered = (
        lax.all_gather(entry_weight.astype(jnp.bfloat16), ("dp", "tensor"), axis=0, tiled=True),
        lax.all_gather(exit_weight.astype(jnp.bfloat16), ("dp", "tensor"), axis=0, tiled=True),
        lax.all_gather(align_weight.astype(jnp.bfloat16), ("dp", "tensor"), axis=0, tiled=True),
        lax.all_gather(position_table.astype(jnp.bfloat16), ("dp", "tensor"), axis=0, tiled=True),
        lax.all_gather(norm_params.astype(jnp.bfloat16), ("dp", "tensor"), axis=0, tiled=True),
    )
    expand_low, reduce_low = (
        lax.all_gather(expand_weight.astype(jnp.bfloat16), "dp", axis=0, tiled=True),
        lax.all_gather(reduce_weight.astype(jnp.bfloat16), "dp", axis=0, tiled=True),
    )
    entry_low = gathered[0].reshape(model_width, 3 * model_width)
    exit_low = gathered[1].reshape(model_width, model_width)
    align_low = gathered[2].reshape(model_width, align_width)
    table_low = gathered[3].reshape(-1, model_width)
    norm_low = gathered[4].astype(jnp.float32).reshape(4, model_width)
    residual = tokens.astype(jnp.float32) + jnp.take(table_low, kept_patches, axis=0).astype(
        jnp.float32
    )
    normed_one = layer_norm(residual, norm_low[0], norm_low[1]).astype(jnp.bfloat16)
    joint_low = jnp.dot(normed_one, entry_low, preferred_element_type=jnp.float32).astype(
        jnp.bfloat16
    )
    split_heads = joint_low.reshape(row_count, 3, H, HD).transpose(1, 2, 0, 3)
    head_outputs, log_totals = lax.map(
        lambda entries: head_forward(entries[0], entries[1], entries[2], same_clip, score_scale),
        (split_heads[0], split_heads[1], split_heads[2]),
    )
    attended = head_outputs.transpose(1, 0, 2).reshape(row_count, model_width).astype(jnp.bfloat16)
    middle = residual + jnp.dot(attended, exit_low, preferred_element_type=jnp.float32)
    normed_two = layer_norm(middle, norm_low[2], norm_low[3]).astype(jnp.bfloat16)
    hidden_in = lax.all_gather(normed_two, "tensor", axis=0, tiled=True)
    hidden_pre = contract(hidden_in, expand_low, 1, 1)
    hidden_act = gelu_exact(hidden_pre).astype(jnp.bfloat16)
    feed_out = lax.psum_scatter(
        jnp.dot(hidden_act, reduce_low, preferred_element_type=jnp.float32).astype(jnp.bfloat16),
        "tensor",
        scatter_dimension=0,
        tiled=True,
    ).astype(jnp.float32)
    out_low = (middle + feed_out).astype(jnp.bfloat16)
    block_out = jnp.where(valid_column, out_low, jnp.zeros_like(out_low))
    align_rows = jnp.dot(out_low, align_low, preferred_element_type=jnp.float32).astype(
        jnp.bfloat16
    )
    aligned = jnp.where(valid_column, align_rows, jnp.zeros_like(align_rows))
    cot_align_valid = jnp.where(valid_column, cot_aligned, jnp.zeros_like(cot_aligned))
    grad_align = contract(out_low, cot_align_valid, 0, 0)
    grad_out = jnp.where(valid_column, cot_output.astype(jnp.float32), 0.0) + contract(
        cot_align_valid, align_low, 1, 1
    )
    grad_feed = grad_out.astype(jnp.bfloat16)
    grad_feed_rows = lax.all_gather(grad_feed, "tensor", axis=0, tiled=True)
    grad_act = contract(grad_feed_rows, reduce_low, 1, 1)
    gelu_value, gelu_back = jax.vjp(gelu_exact, hidden_pre)
    grad_pre = gelu_back(grad_act)[0].astype(jnp.bfloat16)
    grad_reduce = contract(hidden_act, grad_feed_rows, 0, 0)
    grad_expand = contract(grad_pre, hidden_in, 0, 0)
    grad_two = lax.psum_scatter(
        jnp.dot(grad_pre, expand_low, preferred_element_type=jnp.float32),
        "tensor",
        scatter_dimension=0,
        tiled=True,
    )
    grad_expand, grad_reduce = (
        lax.psum_scatter(grad_expand, "dp", scatter_dimension=0, tiled=True),
        lax.psum_scatter(grad_reduce, "dp", scatter_dimension=0, tiled=True),
    )
    norm_value, norm_back_two = jax.vjp(layer_norm, middle, norm_low[2], norm_low[3])
    grad_from_two, grad_gain_two, grad_shift_two = norm_back_two(grad_two)
    grad_middle = grad_out + grad_from_two
    grad_branch = grad_middle.astype(jnp.bfloat16)
    grad_exit = contract(attended, grad_branch, 0, 0)
    grad_attended = contract(grad_branch, exit_low, 1, 1).astype(jnp.bfloat16)
    grad_heads = grad_attended.reshape(row_count, H, HD).transpose(1, 0, 2)
    grad_queries, grad_keys, grad_values = lax.map(
        lambda entries: head_backward(
            entries[0], entries[1], entries[2], entries[3], entries[4], same_clip, score_scale
        ),
        (split_heads[0], split_heads[1], split_heads[2], log_totals, grad_heads),
    )
    grad_joint = jnp.stack((grad_queries, grad_keys, grad_values)).transpose(2, 0, 1, 3)
    grad_joint = grad_joint.reshape(row_count, 3 * model_width).astype(jnp.bfloat16)
    grad_entry = contract(normed_one, grad_joint, 0, 0)
    grad_one = contract(grad_joint, entry_low, 1, 1)
    norm_value_one, norm_back_one = jax.vjp(layer_norm, residual, norm_low[0], norm_low[1])
    grad_from_one, grad_gain_one, grad_shift_one = norm_back_one(grad_one)
    token_grad = grad_middle + grad_from_one
    grad_table = jax.ops.segment_sum(token_grad, kept_patches, num_segments=table_low.shape[0])
    grad_norms = jnp.concatenate((grad_gain_one, grad_shift_one, grad_gain_two, grad_shift_two))
    summed = (
        lax.psum_scatter(grad_entry.reshape(-1), ("dp", "tensor"), scatter_dimension=0, tiled=True),
        lax.psum_scatter(grad_exit.reshape(-1), ("dp", "tensor"), scatter_dimension=0, tiled=True),
        lax.psum_scatter(grad_align.reshape(-1), ("dp", "tensor"), scatter_dimension=0, tiled=True),
        lax.psum_scatter(grad_table.reshape(-1), ("dp", "tensor"), scatter_dimension=0, tiled=True),
        lax.psum_scatter(grad_norms, ("dp", "tensor"), scatter_dimension=0, tiled=True),
    )
    gradients = (summed[0], summed[1], summed[2], grad_expand, grad_reduce, summed[3], summed[4])
    firsts = (
        entry_first,
        exit_first,
        align_first,
        expand_first,
        reduce_first,
        position_first,
        norm_first,
    )
    seconds = (
        entry_second,
        exit_second,
        align_second,
        expand_second,
        reduce_second,
        position_second,
        norm_second,
    )
    decays = (DECAY, DECAY, DECAY, DECAY, DECAY, DECAY, 0.0)
    results = [
        lamb_moments(
            masters[member], gradients[member], firsts[member], seconds[member], decays[member]
        )
        for member in range(7)
    ]
    update_local = jnp.stack([jnp.sum(found[2] * found[2]) for found in results])
    weight_squares, update_squares = lax.psum(
        (jnp.stack([jnp.sum(master * master) for master in masters]), update_local),
        ("dp", "tensor"),
    )
    trust = jnp.sqrt(weight_squares) / jnp.sqrt(update_squares + TINY)
    outputs = [block_out, aligned, token_grad]
    for member in range(7):
        found = results[member]
        outputs = outputs + [found[0], found[1], masters[member] - RATE * trust[member] * found[2]]
    lamb_stats = jnp.stack((trust, jnp.sqrt(weight_squares), jnp.sqrt(update_squares)))
    outputs = outputs + [lamb_stats]
    return tuple(outputs)


def solution(mesh):
    placed = (
        P(("dp", "tensor"), None),
        P(("dp", "tensor")),
        P(),
        P(),
        P(("dp", "tensor"), None),
        P(("dp", "tensor"), None),
        P(("dp", "tensor")),
        P(("dp", "tensor")),
        P(("dp", "tensor")),
        P(("dp", "tensor")),
        P(("dp", "tensor")),
        P(("dp", "tensor")),
        P(("dp", "tensor")),
        P(("dp", "tensor")),
        P(("dp", "tensor")),
        P(("dp", "tensor"), None),
        P(("dp", "tensor"), None),
        P(("dp", "tensor"), None),
        P(("dp", "tensor"), None),
        P(("dp", "tensor"), None),
        P(("dp", "tensor"), None),
        P(("dp", "tensor")),
        P(("dp", "tensor")),
        P(("dp", "tensor")),
        P(("dp", "tensor")),
        P(("dp", "tensor")),
        P(("dp", "tensor")),
    )
    return jax.shard_map(
        local,
        mesh=mesh,
        in_specs=placed,
        out_specs=(
            P(("dp", "tensor"), None),
            P(("dp", "tensor"), None),
            P(("dp", "tensor"), None),
            P(("dp", "tensor")),
            P(("dp", "tensor")),
            P(("dp", "tensor")),
            P(("dp", "tensor")),
            P(("dp", "tensor")),
            P(("dp", "tensor")),
            P(("dp", "tensor")),
            P(("dp", "tensor")),
            P(("dp", "tensor")),
            P(("dp", "tensor"), None),
            P(("dp", "tensor"), None),
            P(("dp", "tensor"), None),
            P(("dp", "tensor"), None),
            P(("dp", "tensor"), None),
            P(("dp", "tensor"), None),
            P(("dp", "tensor")),
            P(("dp", "tensor")),
            P(("dp", "tensor")),
            P(("dp", "tensor")),
            P(("dp", "tensor")),
            P(("dp", "tensor")),
            P(),
        ),
        check_vma=False,
    )
```

profile of v0, /device:TPU:0, one launch (start us, length us, event | category | flops | bytes accessed | tf_op | source)
XLA Modules:
  0.0 1165.3 jit_solution(5532540820435427545)
XLA Ops:
  19.3 42.3 %all-reduce = bf16[3072]{0:T(1024)(128)(2,1)S(1)} all-reduce(bf16[3072]{0:T(1024)(128)(2,1)S(1)} %dynamic-update-slice), channel_id=1, replica_groups=mesh['dp'=16,'tensor'=2] {'dp','tensor'}, use_global_device_ids=true, to_apply=%add | all-reduce | flops 3072 | bytes 12288
  64.1 4.3 all-gather.12.cloned.1.call-done
  71.7 63.2 %all-gather.24.cloned.1.call-done = bf16[32,1,37632]{2,1,0:T(2,128)(2,1)} async-done(((bf16[1,1,37632]{2,1,0:T(2,128)(2,1)}), bf16[32,1,37632]{2,1,0:T(2,128)(2,1)}) %all-gather.24.cloned.1.call-update) | async-done | bytes 2408464 | tf_op jit(solution)/shard_map/all_gather | solution.py:130
  135.0 51.2 %reduce.1 = bf16[32,37632]{1,0:T(8,128)(2,1)} reduce(bf16[32,1,37632]{2,1,0:T(2,128)(2,1)} %all-gather.24.cloned.1.call-done, bf16[]{:T(256)} %constant.226), dimensions={1}, to_apply=%all-gather.reduce_sub_computation | reduce | bytes 4816898 | tf_op jit(solution)/shard_map/all_gather | solution.py:130
  186.1 5.0 reshape.244
  197.4 7.6 reshape.245
  205.0 7.2 convolution_convert_fusion
  212.2 5.8 copy.127
  221.2 3.7 copy.129
  230.9 64.8 %while.28 = (s32[]{:T(128)}, bf16[12,768,64]{1,2,0:T(8,128)(2,1)}, f32[12,768]{1,0:T(8,128)}, bf16[12,768,64]{2,1,0:T(8,128)(2,1)}, bf16[12,768,64]{2,1,0:T(8,12...) while((s32[]{:T(128)}, bf16[12,768,64]{1,2,0:T(8,128)(2,1)}, ...), condition=%wide.region_8.9_spmd.clone, body=%wide.region_5.8_spmd.clone.sunk | while | flops 156302592 | bytes 7911521 | solution.py:150
  308.2 5.2 fusion.90
  313.5 5.4 all-gather.16.cloned.1.call-done
  318.9 11.2 all-gather.14.cloned.1.call-done
  330.1 27.0 %multiply_convert_fusion.1 = (bf16[1536,1536]{1,0:T(8,128)(2,1)}, f32[1536,1536]{1,0:T(8,128)}, f32[1536,1536]{1,0:T(8,128)}) fusion(bf16[1536,768]{0,1:T(8,128)(2,1)} %all-gather.14.cloned.1.call-done, bf16[1536,768]{1,0:T(8,128)(2,1)} %all-gather.16.cloned.1.call-done), kind=kOutput, calls=%fused_computation.57 | convolution fusion | flops 3777232896 | bytes 28311552 | tf_op jit(solution)/shard_map/dot_general | solution.py:19
  357.1 9.2 fusion.95
  366.4 138.8 %reduce-scatter.11.cloned.1.call-done = f32[96,768]{1,0:T(8,128)} async-done(((f32[1536,768]{1,0:T(8,128)}), f32[96,768]{1,0:T(8,128)}) %reduce-scatter.11.cloned.1.call-update) | async-done | bytes 294928 | tf_op jit(solution)/shard_map/reduce_scatter | solution.py:192
  508.0 62.5 %all-gather.18.cloned.1.call-done = bf16[1536,768]{1,0:T(8,128)(2,1)} async-done(((bf16[96,768]{1,0:T(8,128)(2,1)}), bf16[1536,768]{1,0:T(8,128)(2,1)}) %all-gather.18.cloned.1.call-update) | async-done | bytes 2359312 | tf_op jit(solution)/shard_map/all_gather | solution.py:135
  570.5 8.5 convolution_convert_fusion.1
  579.0 14.0 %add_convert_fusion = bf16[1536,1536]{1,0:T(8,128)(2,1)S(1)} fusion(f32[1536,1536]{1,0:T(8,128)} %get-tuple-element.433, bf16[1536,768]{0,1:T(8,128)(2,1)} %all-gather.22.cloned.1.call-done, bf16[1536,768]{1,0:T(8,128)(2,1)} %all-gather.18.cloned.1.call-done, f32[1536,1536]{1,0:T(8,128)} %get-tuple-element.462), kind=kOutput, calls=%fused_computation.56 | convolution fusion | flops 3656908800 | bytes 28311552 | tf_op jit(solution)/shard_map/dot_general | solution.py:19
  595.2 5.7 fusion.92
  601.5 9.4 fusion.94
  629.6 107.8 %while.29 = (s32[]{:T(128)}, bf16[12,768,64]{1,2,0:T(8,128)(2,1)S(1)}, bf16[12,768,64]{1,2,0:T(8,128)(2,1)}, bf16[12,768,64]{1,2,0:T(8,128)(2,1)}, bf16[12,768,6...) while((s32[]{:T(128)}, ...), condition=%wide.region_17.18_spmd.clone, body=%wide.region_15.17_spmd.clone.sunk | while | flops 383483136 | bytes 19690608 | solution.py:201
  745.7 5.5 fusion.76
  751.2 7.9 reshape.252
  759.1 7.4 fusion.91
  779.4 9.9 scatter_custom_fusion
  789.3 5.9 reshape.255
  799.7 41.4 %all-reduce.5 = f32[3072]{0:T(1024)S(1)} all-reduce(f32[3072]{0:T(1024)S(1)} %pad_maximum_fusion), channel_id=10, replica_groups=mesh['dp'=16,'tensor'=2] {'dp','tensor'}, use_global_device_ids=true, to_apply=%region_45.46.clone | all-reduce | flops 3072 | bytes 24576
  844.6 239.9 %all-reduce.10.cloned.1.call-done = (f32[1769472]{0:T(1024)}, f32[589824]{0:T(1024)}, f32[786432]{0:T(1024)}, f32[1204224]{0:T(1024)}) async-done(((f32[1769472]{0:T(1024)}, f32[589824]{0:T(1024)}, f32[786432]{0:T(1024)}, f32[1204224]{0:T(1024)}), (f32[1769472]{0:T(1024)}, f32[589824]{0:T(1024)}, f32[786432]{0:T(1024)}, f32[1204224]{0:T(1024)})) %all-reduce.10.cloned.1.call-update) | async-done | bytes 17399824
  1094.1 4.5 stack.83
  1098.7 4.6 stack.91
  1104.7 39.6 %all-reduce.6 = (f32[7]{0:T(128)S(1)}, f32[7]{0:T(128)S(1)}) all-reduce(f32[7]{0:T(128)S(1)} %stack.91, f32[7]{0:T(128)S(1)} %stack.83), channel_id=1, replica_groups=mesh['dp'=16,'tensor'=2] {'dp','tensor'}, use_global_device_ids=true, to_apply=%region_47.48 | all-reduce | flops 14 | bytes 112 | tf_op jit(solution)/shard_map/psum | solution.py:250
  (412 shorter events, 291.6 us)
Async XLA Ops:
  7.2 61.2 %all-gather.12.cloned.1.call-start = ((), (), s32[]{:S(2)}) async-start(), calls=%async_computation.5 | async-start | bytes 1216512 | tf_op jit(solution)/shard_map/all_gather | solution.py:128
  8.9 126.1 %all-gather.24.cloned.1.call-start = ((), (), s32[]{:S(2)}) async-start(), calls=%async_computation.15 | async-start | bytes 4967424 | tf_op jit(solution)/shard_map/all_gather | solution.py:130
  10.6 186.7 %all-gather.10.cloned.1.call-start = ((), (), s32[]{:S(2)}) async-start(), calls=%async_computation.4 | async-start | bytes 3649536 | tf_op jit(solution)/shard_map/all_gather | solution.py:127
  12.3 292.2 %all-gather.20.cloned.1.call-start = ((), (), s32[]{:S(2)}) async-start(), calls=%async_computation.10 | async-start | bytes 1622016 | tf_op jit(solution)/shard_map/all_gather | solution.py:129
  13.9 305.0 %all-gather.16.cloned.1.call-start = ((), (), s32[]{:S(2)}) async-start(), calls=%async_computation.7 | async-start | bytes 2506752 | tf_op jit(solution)/shard_map/all_gather | solution.py:134
  15.6 314.5 %all-gather.14.cloned.1.call-start = ((), (), s32[]{:S(2)}) async-start(), calls=%async_computation.6 | async-start | bytes 3538944 | tf_op jit(solution)/shard_map/all_gather | solution.py:157
  17.1 187.9 %copy-start.51 = (pred[768]{0:T(1024)(128)(4,1)}, pred[768]{0:T(1024)(128)(4,1)S(1)}, u32[]{:S(2)}) copy-start(pred[768]{0:T(1024)(128)(4,1)S(1)} %compare_and_fusion) | copy-start | bytes 2308
  62.2 142.8 %copy-start.43 = (f32[768]{0:T(1024)}, f32[768]{0:T(1024)S(1)}, u32[]{:S(2)}) copy-start(f32[768]{0:T(1024)S(1)} %get-tuple-element.446) | copy-start | bytes 9220
  62.2 142.8 %copy-start.57 = (f32[768]{0:T(1024)}, f32[768]{0:T(1024)S(1)}, u32[]{:S(2)}) copy-start(f32[768]{0:T(1024)S(1)} %get-tuple-element.447) | copy-start | bytes 9220
  301.3 55.8 %all-gather.22.cloned.1.call-start = ((), (), s32[]{:S(2)}) async-start(), calls=%async_computation.11 | async-start | bytes 3538944 | tf_op jit(solution)/shard_map/all_gather | solution.py:178
  313.4 191.8 %reduce-scatter.11.cloned.1.call-start = ((), (), s32[]{:S(2)}) async-start(), calls=%async_computation.14 | async-start | bytes 5013504 | tf_op jit(solution)/shard_map/reduce_scatter | solution.py:192
  366.3 138.9 %copy-start.22 = (f32[96,768]{1,0:T(8,128)S(1)}, f32[96,768]{1,0:T(8,128)}, u32[]{:S(2)}) copy-start(f32[96,768]{1,0:T(8,128)} %param.49) | copy-start | bytes 884740
  366.3 138.9 %copy-start.32 = (f32[96,768]{1,0:T(8,128)S(1)}, f32[96,768]{1,0:T(8,128)}, u32[]{:S(2)}) copy-start(f32[96,768]{1,0:T(8,128)} %param.51) | copy-start | bytes 884740
  366.3 138.9 %copy-start.33 = (f32[96,768]{1,0:T(8,128)S(1)}, f32[96,768]{1,0:T(8,128)}, u32[]{:S(2)}) copy-start(f32[96,768]{1,0:T(8,128)} %param.50) | copy-start | bytes 884740
  366.4 204.1 %all-gather.18.cloned.1.call-start = ((), (), s32[]{:S(2)}) async-start(), calls=%async_computation.8 | async-start | bytes 2506752 | tf_op jit(solution)/shard_map/all_gather | solution.py:135
  507.8 103.2 %reduce-scatter.5.cloned.1.call-start = ((), (), s32[]{:S(2)}) async-start(), calls=%async_computation.9 | async-start | bytes 3538944 | tf_op jit(solution)/shard_map/reduce_scatter | solution.py:160
  579.0 39.3 %reduce-scatter.7.cloned.1.call-start = ((), (), s32[]{:S(2)}) async-start(), calls=%async_computation.12 | async-start | bytes 7077888 | tf_op jit(solution)/shard_map/reduce_scatter | solution.py:184
  601.0 241.4 %reduce-scatter.9.cloned.1.call-start = ((), (), s32[]{:S(2)}) async-start(), calls=%async_computation.13 | async-start | bytes 5013504 | tf_op jit(solution)/shard_map/reduce_scatter | solution.py:191
  610.9 473.7 %all-reduce.10.cloned.1.call-start = ((), (), s32[]{:S(2)}) async-start(), calls=%async_computation.16 | async-start | bytes 34799616
  797.0 287.6 %copy-start.14 = (f32[55296]{0:T(1024)S(1)}, f32[55296]{0:T(1024)}, u32[]{:S(2)}) copy-start(f32[55296]{0:T(1024)} %param.37) | copy-start | bytes 663556
  799.6 287.6 %copy-start.16 = (f32[37632]{0:T(1024)S(1)}, f32[37632]{0:T(1024)}, u32[]{:S(2)}) copy-start(f32[37632]{0:T(1024)} %param.52) | copy-start | bytes 451588
  799.6 287.6 %copy-start.34 = (f32[37632]{0:T(1024)S(1)}, f32[37632]{0:T(1024)}, u32[]{:S(2)}) copy-start(f32[37632]{0:T(1024)} %param.54) | copy-start | bytes 451588
  799.6 287.6 %copy-start.35 = (f32[37632]{0:T(1024)S(1)}, f32[37632]{0:T(1024)}, u32[]{:S(2)}) copy-start(f32[37632]{0:T(1024)} %param.53) | copy-start | bytes 451588
  799.6 290.1 %copy-start.30 = (f32[24576]{0:T(1024)S(1)}, f32[24576]{0:T(1024)}, u32[]{:S(2)}) copy-start(f32[24576]{0:T(1024)} %param.43) | copy-start | bytes 294916
  799.6 290.1 %copy-start.38 = (f32[24576]{0:T(1024)S(1)}, f32[24576]{0:T(1024)}, u32[]{:S(2)}) copy-start(f32[24576]{0:T(1024)} %param.45) | copy-start | bytes 294916
  799.6 290.1 %copy-start.39 = (f32[24576]{0:T(1024)S(1)}, f32[24576]{0:T(1024)}, u32[]{:S(2)}) copy-start(f32[24576]{0:T(1024)} %param.44) | copy-start | bytes 294916
  799.6 292.3 %copy-start.31 = (f32[18432]{0:T(1024)S(1)}, f32[18432]{0:T(1024)}, u32[]{:S(2)}) copy-start(f32[18432]{0:T(1024)} %param.40) | copy-start | bytes 221188
  799.7 292.3 %copy-start.40 = (f32[18432]{0:T(1024)S(1)}, f32[18432]{0:T(1024)}, u32[]{:S(2)}) copy-start(f32[18432]{0:T(1024)} %param.42) | copy-start | bytes 221188
  799.7 292.3 %copy-start.41 = (f32[18432]{0:T(1024)S(1)}, f32[18432]{0:T(1024)}, u32[]{:S(2)}) copy-start(f32[18432]{0:T(1024)} %param.41) | copy-start | bytes 221188
  842.4 260.9 %copy-start.10 = (bf16[768,768]{0,1:T(8,128)(2,1)S(1)}, bf16[768,768]{0,1:T(8,128)(2,1)}, u32[]{:S(2)}) copy-start(bf16[768,768]{0,1:T(8,128)(2,1)} %get-tuple-element.430) | copy-start | bytes 3538948
  844.6 312.8 %copy-start.28 = (f32[96,768]{1,0:T(8,128)}, f32[96,768]{1,0:T(8,128)S(1)}, u32[]{:S(2)}) copy-start(f32[96,768]{1,0:T(8,128)S(1)} %get-tuple-element.420) | copy-start | bytes 884740
  844.6 312.8 %copy-start.29 = (f32[96,768]{1,0:T(8,128)}, f32[96,768]{1,0:T(8,128)S(1)}, u32[]{:S(2)}) copy-start(f32[96,768]{1,0:T(8,128)S(1)} %get-tuple-element.421) | copy-start | bytes 884740
  (51 other events, 639.5 us)
Sparse Core Ops, SparseCore 0:
  11.6 56.8 all-gather.11
  71.8 63.1 all-gather.23
  138.4 58.8 all-gather.9
  200.6 53.7 all-gather.19
  257.7 61.1 all-gather.15
  320.3 9.7 all-gather.13
  331.6 12.1 all-gather.21
  366.5 138.6 reduce-scatter.10
  508.9 61.4 all-gather.17
  579.1 8.7 reduce-scatter.4
  601.1 11.3 reduce-scatter.6
  618.4 138.7 reduce-scatter.8
  795.4 289.1 all-reduce.9
where the time goes:
time: 1180 us; the launch traced here: 1170 us
  waiting for transfers between devices  526 us (45%)
  matrix products  248 us (21%)
  other arithmetic  125 us (11%)
  blocking collectives  123 us (10%)
  local copies, waits for them, and re-layouts  122 us (10%)
  between operations  19.4 us (2%)
    unnamed x14, waiting for transfers between devices  240 us
    dot_general x70, matrix products, contract(): lax.dot_general(left, right, (((left_dim,), (right_dim,)), ((), ())), pre...  180 us
    reduce_scatter x1, waiting for transfers between devices, local(): lax.psum_scatter(grad_reduce, 'dp', scatter_dimension=0, tiled=True)  139 us
    unnamed x2, blocking collectives  83.7 us
    all_gather x1, waiting for transfers between devices, local(): lax.all_gather(position_table.astype(jnp.bfloat16), ('dp', 'tensor'), axi...  63.2 us
    all_gather x1, waiting for transfers between devices, local(): lax.all_gather(reduce_weight.astype(jnp.bfloat16), 'dp', axis=0, tiled=True)  62.5 us
    all_gather x1, other arithmetic, local(): lax.all_gather(position_table.astype(jnp.bfloat16), ('dp', 'tensor'), axi...  51.2 us
    psum x1, blocking collectives, local(): lax.psum((jnp.stack([jnp.sum(master * master) for master in masters]), up...  39.6 us
  transfers between devices with their start and end apart: 13, of which 7 were waited for; matrix products, arithmetic and copies ran while one was open for 37% of the time, Pallas kernels for 0%

commit v1 on v0

--- a/solution.py
+++ b/solution.py
@@ -13,6 +13,29 @@
 ADAM_EPS = 1e-06
 DECAY = 0.05
 TINY = 1e-06
+
+
+def in_order(blocks, dim):
+    blocks = jnp.moveaxis(blocks, 0, dim)
+    dims = blocks.shape
+    return blocks.reshape(*dims[:dim], dims[dim] * dims[dim + 1], *dims[dim + 2 :])
+
+
+def doubled(shard, axis):
+    devices, index = (lax.axis_size(axis), lax.axis_index(axis))
+    tiles, bit = (shard[None], 1)
+    while bit < devices:
+        partner_block = lax.ppermute(tiles, axis, [(i, i ^ bit) for i in range(devices)])
+        low = index & bit == 0
+        tiles = jnp.concatenate(
+            [jnp.where(low, tiles, partner_block), jnp.where(low, partner_block, tiles)]
+        )
+        bit *= 2
+    return tiles
+
+
+def gather_by_bits(x, axis, dim):
+    return in_order(doubled(x, axis), dim)
 
 
 def contract(left, right, left_dim, right_dim):
@@ -127,7 +150,7 @@
         lax.all_gather(entry_weight.astype(jnp.bfloat16), ("dp", "tensor"), axis=0, tiled=True),
         lax.all_gather(exit_weight.astype(jnp.bfloat16), ("dp", "tensor"), axis=0, tiled=True),
         lax.all_gather(align_weight.astype(jnp.bfloat16), ("dp", "tensor"), axis=0, tiled=True),
-        lax.all_gather(position_table.astype(jnp.bfloat16), ("dp", "tensor"), axis=0, tiled=True),
+        gather_by_bits(position_table.astype(jnp.bfloat16), ("dp", "tensor"), 0),
         lax.all_gather(norm_params.astype(jnp.bfloat16), ("dp", "tensor"), axis=0, tiled=True),
     )
     expand_low, reduce_low = (

time: 1180 us -> 1130 us (0.958)
  other arithmetic: 125 us -> 77 us
  waiting for transfers between devices: 526 us -> 488 us
  blocking collectives: 123 us -> 156 us
    all_gather x1 -> x0, waiting for transfers between devices: 63.2 us -> none  [local(): lax.all_gather(position_table.astype(jnp.bfloat16), ('dp', 'tensor'), axi...]
    all_gather x1 -> x0, other arithmetic: 51.2 us -> none  [local(): lax.all_gather(position_table.astype(jnp.bfloat16), ('dp', 'tensor'), axi...]
    unnamed x2, blocking collectives: 83.7 us -> 116 us
    ppermute x0 -> x5, waiting for transfers between devices: none -> 23.1 us  [doubled(): lax.ppermute(tiles, axis, [(i, i ^ bit) for i in range(devices)])]
    unnamed x151 -> x152, local copies, waits for them, and re-layouts: 29.1 us -> 28.9 us
    unnamed x14 -> x13, waiting for transfers between devices: 240 us -> 240 us
  transfers between devices with their start and end apart: 13 -> 17, of which waited for: 7 -> 9; matrix products, arithmetic and copies ran while one was open for 37% -> 34% of each run, Pallas kernels for 0% -> 0%
where the time goes in v1:
time: 1130 us; the launch traced here: 1120 us
  waiting for transfers between devices  488 us (43%)
  matrix products  247 us (22%)
  blocking collectives  156 us (14%)
  local copies, waits for them, and re-layouts  122 us (11%)
  other arithmetic  77 us (7%)
  between operations  19.8 us (2%)
    unnamed x13, waiting for transfers between devices  240 us
    dot_general x70, matrix products, contract(): lax.dot_general(left, right, (((left_dim,), (right_dim,)), ((), ())), pre...  179 us
    reduce_scatter x1, waiting for transfers between devices, local(): lax.psum_scatter(grad_reduce, 'dp', scatter_dimension=0, tiled=True)  139 us
    unnamed x2, blocking collectives  116 us
    all_gather x1, waiting for transfers between devices, local(): lax.all_gather(reduce_weight.astype(jnp.bfloat16), 'dp', axis=0, tiled=True)  62.6 us
    psum x1, blocking collectives, local(): lax.psum((jnp.stack([jnp.sum(master * master) for master in masters]), up...  39.6 us
    unnamed x152, local copies, waits for them, and re-layouts  28.9 us
    dot_general x12, matrix products, head_forward(): jnp.dot(attention.astype(jnp.bfloat16), value_rows, preferred_element_typ...  25.3 us
  transfers between devices with their start and end apart: 17, of which 9 were waited for; matrix products, arithmetic and copies ran while one was open for 34% of the time, Pallas kernels for 0%

profile of v1, /device:TPU:0, one launch (start us, length us, event | category | flops | bytes accessed | tf_op | source)
XLA Modules:
  0.0 1120.9 jit_solution(12619148393765771249)
XLA Ops:
  23.3 6.7 collective-permute-done.2
  33.1 13.4 %collective-permute-done.3 = bf16[8,37632]{1,0:T(8,128)(2,1)S(1)} collective-permute-done((bf16[8,37632]{1,0:T(8,128)(2,1)S(1)}, bf16[8,37632]{1,0:T(8,128)(2,1)S(1)}, u32[]{:S(2)}, u32[]{:S(2)}) %collective-permute-start.3) | collective-permute-done | bytes 602144 | tf_op jit(solution)/shard_map/ppermute | solution.py:28
  54.2 74.4 %all-reduce = bf16[3072]{0:T(1024)(128)(2,1)S(1)} all-reduce(bf16[3072]{0:T(1024)(128)(2,1)S(1)} %dynamic-update-slice), channel_id=1, replica_groups=mesh['dp'=16,'tensor'=2] {'dp','tensor'}, use_global_device_ids=true, to_apply=%add | all-reduce | flops 3072 | bytes 12288
  135.5 5.0 reshape_reshape.3
  146.7 6.2 all-gather.8.cloned.1.call-done
  152.9 7.6 reshape.241
  160.5 6.7 convolution_convert_fusion
  167.2 5.8 copy.107
  176.3 3.7 copy.109
  185.9 64.9 %while.28 = (s32[]{:T(128)}, bf16[12,768,64]{1,2,0:T(8,128)(2,1)}, f32[12,768]{1,0:T(8,128)}, bf16[12,768,64]{2,1,0:T(8,128)(2,1)}, bf16[12,768,64]{2,1,0:T(8,12...) while((s32[]{:T(128)}, bf16[12,768,64]{1,2,0:T(8,128)(2,1)}, ...), condition=%wide.region_8.9_spmd.clone, body=%wide.region_5.8_spmd.clone.sunk | while | flops 156302592 | bytes 7911521 | solution.py:173
  263.0 5.2 fusion.90
  268.3 6.3 all-gather.14.cloned.1.call-done
  274.5 11.2 all-gather.12.cloned.1.call-done
  285.7 26.9 %multiply_convert_fusion.1 = (bf16[1536,1536]{1,0:T(8,128)(2,1)}, f32[1536,1536]{1,0:T(8,128)}, f32[1536,1536]{1,0:T(8,128)}) fusion(bf16[1536,768]{0,1:T(8,128)(2,1)} %all-gather.12.cloned.1.call-done, bf16[1536,768]{1,0:T(8,128)(2,1)} %all-gather.14.cloned.1.call-done), kind=kOutput, calls=%fused_computation.57 | convolution fusion | flops 3777232896 | bytes 28311552 | tf_op jit(solution)/shard_map/dot_general | solution.py:42
  312.6 9.2 fusion.95
  322.1 138.6 %reduce-scatter.11.cloned.1.call-done = f32[96,768]{1,0:T(8,128)} async-done(((f32[1536,768]{1,0:T(8,128)}), f32[96,768]{1,0:T(8,128)}) %reduce-scatter.11.cloned.1.call-update) | async-done | bytes 294928 | tf_op jit(solution)/shard_map/reduce_scatter | solution.py:215
  463.3 62.6 %all-gather.16.cloned.1.call-done = bf16[1536,768]{1,0:T(8,128)(2,1)} async-done(((bf16[96,768]{1,0:T(8,128)(2,1)}), bf16[1536,768]{1,0:T(8,128)(2,1)}) %all-gather.16.cloned.1.call-update) | async-done | bytes 2359312 | tf_op jit(solution)/shard_map/all_gather | solution.py:158
  526.0 8.5 convolution_convert_fusion.1
  534.5 14.0 %add_convert_fusion = bf16[1536,1536]{1,0:T(8,128)(2,1)S(1)} fusion(f32[1536,1536]{1,0:T(8,128)} %get-tuple-element.391, bf16[1536,768]{0,1:T(8,128)(2,1)} %all-gather.20.cloned.1.call-done, bf16[1536,768]{1,0:T(8,128)(2,1)} %all-gather.16.cloned.1.call-done, f32[1536,1536]{1,0:T(8,128)} %get-tuple-element.430), kind=kOutput, calls=%fused_computation.56 | convolution fusion | flops 3656908800 | bytes 28311552 | tf_op jit(solution)/shard_map/dot_general | solution.py:42
  550.7 5.7 fusion.92
  556.9 9.4 fusion.94
  585.0 107.6 %while.29 = (s32[]{:T(128)}, bf16[12,768,64]{1,2,0:T(8,128)(2,1)S(1)}, bf16[12,768,64]{1,2,0:T(8,128)(2,1)}, bf16[12,768,64]{1,2,0:T(8,128)(2,1)}, bf16[12,768,6...) while((s32[]{:T(128)}, ...), condition=%wide.region_17.18_spmd.clone, body=%wide.region_15.17_spmd.clone.sunk | while | flops 383483136 | bytes 19690608 | solution.py:224
  700.7 5.5 fusion.76
  706.2 8.0 reshape.248
  714.2 7.4 fusion.91
  734.5 9.9 scatter_custom_fusion
  744.3 5.9 reshape.251
  754.7 41.7 %all-reduce.5 = f32[3072]{0:T(1024)S(1)} all-reduce(f32[3072]{0:T(1024)S(1)} %pad_maximum_fusion.5), channel_id=10, replica_groups=mesh['dp'=16,'tensor'=2] {'dp','tensor'}, use_global_device_ids=true, to_apply=%region_45.46.clone | all-reduce | flops 3072 | bytes 24576
  799.9 239.8 %all-reduce.10.cloned.1.call-done = (f32[1769472]{0:T(1024)}, f32[589824]{0:T(1024)}, f32[786432]{0:T(1024)}, f32[1204224]{0:T(1024)}) async-done(((f32[1769472]{0:T(1024)}, f32[589824]{0:T(1024)}, f32[786432]{0:T(1024)}, f32[1204224]{0:T(1024)}), (f32[1769472]{0:T(1024)}, f32[589824]{0:T(1024)}, f32[786432]{0:T(1024)}, f32[1204224]{0:T(1024)})) %all-reduce.10.cloned.1.call-update) | async-done | bytes 17399824
  1049.3 4.6 stack.83
  1054.0 4.7 stack.91
  1060.1 39.6 %all-reduce.6 = (f32[7]{0:T(128)S(1)}, f32[7]{0:T(128)S(1)}) all-reduce(f32[7]{0:T(128)S(1)} %stack.91, f32[7]{0:T(128)S(1)} %stack.83), channel_id=1, replica_groups=mesh['dp'=16,'tensor'=2] {'dp','tensor'}, use_global_device_ids=true, to_apply=%region_47.48 | all-reduce | flops 14 | bytes 112 | tf_op jit(solution)/shard_map/psum | solution.py:273
  (430 shorter events, 306.4 us)
Async XLA Ops:
  7.2 122.9 %all-gather.10.cloned.1.call-start = ((), (), s32[]{:S(2)}) async-start(), calls=%async_computation.5 | async-start | bytes 1216512 | tf_op jit(solution)/shard_map/all_gather | solution.py:151
  8.8 144.1 %all-gather.8.cloned.1.call-start = ((), (), s32[]{:S(2)}) async-start(), calls=%async_computation.4 | async-start | bytes 3649536 | tf_op jit(solution)/shard_map/all_gather | solution.py:150
  9.9 2.2 collective-permute-start
  12.0 247.3 %all-gather.18.cloned.1.call-start = ((), (), s32[]{:S(2)}) async-start(), calls=%async_computation.10 | async-start | bytes 1622016 | tf_op jit(solution)/shard_map/all_gather | solution.py:152
  12.7 7.1 collective-permute-start.1
  16.8 257.7 %all-gather.14.cloned.1.call-start = ((), (), s32[]{:S(2)}) async-start(), calls=%async_computation.7 | async-start | bytes 2506752 | tf_op jit(solution)/shard_map/all_gather | solution.py:157
  20.7 9.3 collective-permute-start.2
  23.2 262.5 %all-gather.12.cloned.1.call-start = ((), (), s32[]{:S(2)}) async-start(), calls=%async_computation.6 | async-start | bytes 3538944 | tf_op jit(solution)/shard_map/all_gather | solution.py:180
  30.7 15.8 %collective-permute-start.3 = (bf16[8,37632]{1,0:T(8,128)(2,1)S(1)}, bf16[8,37632]{1,0:T(8,128)(2,1)S(1)}, u32[]{:S(2)}, u32[]{:S(2)}) collective-permute-start(bf16[8,37632]{1,0:T(8,128)(2,1)S(1)} %pad_maximum_fusion.2), channel_id=1, source_target_pairs={{0,8},{1,9},{2,10},{3,11},{4,12},{5,13},{6,14},{7,15},{8,0},{9,1},... | collective-permute-start | bytes 1806344 | tf_op jit(solution)/shard_map/ppermute | solution.py:28
  48.0 85.4 %collective-permute-start.4 = (bf16[16,37632]{1,0:T(8,128)(2,1)}, bf16[16,37632]{1,0:T(8,128)(2,1)S(1)}, u32[]{:S(2)}, u32[]{:S(2)}) collective-permute-start(bf16[16,37632]{1,0:T(8,128)(2,1)} %pad_maximum_fusion.1), channel_id=1, source_target_pairs={{0,16},{1,17},{2,18},{3,19},{4,20},{5,21},{6,22},{7,23},{8,24},{9,... | collective-permute-start | bytes 3612680 | tf_op jit(solution)/shard_map/ppermute | solution.py:28
  256.4 56.2 %all-gather.20.cloned.1.call-start = ((), (), s32[]{:S(2)}) async-start(), calls=%async_computation.11 | async-start | bytes 3538944 | tf_op jit(solution)/shard_map/all_gather | solution.py:201
  268.2 192.5 %reduce-scatter.11.cloned.1.call-start = ((), (), s32[]{:S(2)}) async-start(), calls=%async_computation.14 | async-start | bytes 5013504 | tf_op jit(solution)/shard_map/reduce_scatter | solution.py:215
  321.8 138.9 %copy-start.32 = (f32[96,768]{1,0:T(8,128)S(1)}, f32[96,768]{1,0:T(8,128)}, u32[]{:S(2)}) copy-start(f32[96,768]{1,0:T(8,128)} %param.51) | copy-start | bytes 884740
  321.8 138.9 %copy-start.33 = (f32[96,768]{1,0:T(8,128)S(1)}, f32[96,768]{1,0:T(8,128)}, u32[]{:S(2)}) copy-start(f32[96,768]{1,0:T(8,128)} %param.50) | copy-start | bytes 884740
  321.9 204.1 %all-gather.16.cloned.1.call-start = ((), (), s32[]{:S(2)}) async-start(), calls=%async_computation.8 | async-start | bytes 2506752 | tf_op jit(solution)/shard_map/all_gather | solution.py:158
  463.3 103.1 %reduce-scatter.5.cloned.1.call-start = ((), (), s32[]{:S(2)}) async-start(), calls=%async_computation.9 | async-start | bytes 3538944 | tf_op jit(solution)/shard_map/reduce_scatter | solution.py:183
  534.4 39.2 %reduce-scatter.7.cloned.1.call-start = ((), (), s32[]{:S(2)}) async-start(), calls=%async_computation.12 | async-start | bytes 7077888 | tf_op jit(solution)/shard_map/reduce_scatter | solution.py:207
  556.4 241.2 %reduce-scatter.9.cloned.1.call-start = ((), (), s32[]{:S(2)}) async-start(), calls=%async_computation.13 | async-start | bytes 5013504 | tf_op jit(solution)/shard_map/reduce_scatter | solution.py:214
  566.3 473.4 %all-reduce.10.cloned.1.call-start = ((), (), s32[]{:S(2)}) async-start(), calls=%async_computation.15 | async-start | bytes 34799616
  752.0 287.7 %copy-start.15 = (f32[55296]{0:T(1024)S(1)}, f32[55296]{0:T(1024)}, u32[]{:S(2)}) copy-start(f32[55296]{0:T(1024)} %param.37) | copy-start | bytes 663556
  754.6 287.8 %copy-start.17 = (f32[37632]{0:T(1024)S(1)}, f32[37632]{0:T(1024)}, u32[]{:S(2)}) copy-start(f32[37632]{0:T(1024)} %param.52) | copy-start | bytes 451588
  754.6 287.8 %copy-start.34 = (f32[37632]{0:T(1024)S(1)}, f32[37632]{0:T(1024)}, u32[]{:S(2)}) copy-start(f32[37632]{0:T(1024)} %param.54) | copy-start | bytes 451588
  754.6 287.8 %copy-start.35 = (f32[37632]{0:T(1024)S(1)}, f32[37632]{0:T(1024)}, u32[]{:S(2)}) copy-start(f32[37632]{0:T(1024)} %param.53) | copy-start | bytes 451588
  754.6 290.2 %copy-start.30 = (f32[24576]{0:T(1024)S(1)}, f32[24576]{0:T(1024)}, u32[]{:S(2)}) copy-start(f32[24576]{0:T(1024)} %param.43) | copy-start | bytes 294916
  754.6 290.2 %copy-start.38 = (f32[24576]{0:T(1024)S(1)}, f32[24576]{0:T(1024)}, u32[]{:S(2)}) copy-start(f32[24576]{0:T(1024)} %param.45) | copy-start | bytes 294916
  754.6 290.2 %copy-start.39 = (f32[24576]{0:T(1024)S(1)}, f32[24576]{0:T(1024)}, u32[]{:S(2)}) copy-start(f32[24576]{0:T(1024)} %param.44) | copy-start | bytes 294916
  754.7 292.4 %copy-start.31 = (f32[18432]{0:T(1024)S(1)}, f32[18432]{0:T(1024)}, u32[]{:S(2)}) copy-start(f32[18432]{0:T(1024)} %param.40) | copy-start | bytes 221188
  754.7 292.4 %copy-start.40 = (f32[18432]{0:T(1024)S(1)}, f32[18432]{0:T(1024)}, u32[]{:S(2)}) copy-start(f32[18432]{0:T(1024)} %param.42) | copy-start | bytes 221188
  754.7 292.4 %copy-start.41 = (f32[18432]{0:T(1024)S(1)}, f32[18432]{0:T(1024)}, u32[]{:S(2)}) copy-start(f32[18432]{0:T(1024)} %param.41) | copy-start | bytes 221188
  797.7 260.9 %copy-start.10 = (bf16[768,768]{0,1:T(8,128)(2,1)S(1)}, bf16[768,768]{0,1:T(8,128)(2,1)}, u32[]{:S(2)}) copy-start(bf16[768,768]{0,1:T(8,128)(2,1)} %get-tuple-element.388) | copy-start | bytes 3538948
  799.9 312.8 %copy-start.28 = (f32[96,768]{1,0:T(8,128)}, f32[96,768]{1,0:T(8,128)S(1)}, u32[]{:S(2)}) copy-start(f32[96,768]{1,0:T(8,128)S(1)} %get-tuple-element.378) | copy-start | bytes 884740
  799.9 312.8 %copy-start.29 = (f32[96,768]{1,0:T(8,128)}, f32[96,768]{1,0:T(8,128)S(1)}, u32[]{:S(2)}) copy-start(f32[96,768]{1,0:T(8,128)S(1)} %get-tuple-element.379) | copy-start | bytes 884740
  (56 other events, 857.2 us)
Sparse Core Ops, SparseCore 0:
  11.5 75.5 all-gather.9
  90.6 62.2 all-gather.7
  156.3 53.7 all-gather.17
  213.3 61.1 all-gather.13
  275.9 9.7 all-gather.11
  287.1 12.1 all-gather.19
  322.0 138.6 reduce-scatter.10
  464.4 61.4 all-gather.15
  534.6 8.7 reduce-scatter.4
  556.5 11.3 reduce-scatter.6
  574.0 138.6 reduce-scatter.8
  750.4 289.2 all-reduce.9
